TPU v7x, 128 devices: a whole 4x4x4 slice. The times are simulated.
128 devices in a mesh: grp: 4 (over x), blk: 32 (over z, y, core).
Axes of the slice: x: 4, y: 4, z: 4, core: 2. Of those that a mesh axis runs over, the one named last changes fastest.
Arguments:
- activations: bfloat16 [131072, 3072], P(('grp', 'blk')), may hold values from -6 to 6
- out_grads: bfloat16 [131072, 3072], P(('grp', 'blk')), may hold values from -6 to 6
- proj_act: bfloat16 [3072, 128], replicated, may hold values from -1 to 1
- proj_out: bfloat16 [3072, 256], replicated, may hold values from -0.109375 to 0.109375
Outputs:
- scores: float32 [2048, 512], P(('grp', 'blk'))
All inputs are finite; a program needn't handle non-finite values.
Results may differ from a plain program's by a relative error of at most 0.0012.
Values may be sent and summed in bfloat16 or wider, within the bound.
No kernel may reach another device: no remote copies, remote signals or barrier semaphores. Data moves between devices by JAX's collectives and lax.ppermute only.
A program may use at most 64 MiB of HBM per device.

v0:
```python
import math
import jax
import jax.numpy as jnp
from jax import lax
from jax.sharding import Mesh
from jax.sharding import PartitionSpec as P

SEQ = 64
ITERS = 4
BLK = ("blk_0", "blk_1", "blk_2")
GRP_BLK = ("grp", "blk_0", "blk_1", "blk_2")
damping_rate = 0.5
power_steps = 3


def split_up(array, dim, size):
    shape = array.shape
    blocks = array.reshape(*shape[:dim], size, shape[dim] // size, *shape[dim + 1 :])
    return jnp.moveaxis(blocks, dim, 0)


def in_order(blocks, dim):
    shape = list(blocks.shape[1:])
    shape[dim] *= blocks.shape[0]
    return jnp.moveaxis(blocks, 0, dim).reshape(shape)


def moved_by_axis(blocks, axes, turns):
    shape = [lax.axis_size(a) for a in axes]
    blocks = blocks.reshape(*shape, *blocks.shape[1:])
    for k in turns:
        blocks = lax.all_to_all(blocks, axes[k], split_axis=k, concat_axis=k, tiled=True)
    return blocks.reshape(-1, *blocks.shape[len(axes) :])


def core_and_chips(array, groups, turns, split_dim, concat_dim):
    size = lax.axis_size(groups[0]) * lax.axis_size(groups[1])
    blocks = split_up(array, split_dim, size)
    return in_order(moved_by_axis(blocks, groups, turns), concat_dim)


def one_axis_at_a_time(array, axes):
    for axis in axes:
        array = lax.psum(array, axis)
    return array


def sum_at_owner(array, axis, dim):
    size = lax.axis_size(axis)
    blocks = lax.all_to_all(split_up(array, dim, size), axis, 0, 0, tiled=True)
    return jnp.sum(blocks, axis=0)


def top_estimate(gram_sum):
    width = gram_sum.shape[0]
    vector = jnp.full((width,), 1.0 / math.sqrt(width), jnp.float32)
    top = jnp.float32(1.0)
    for step in range(power_steps):
        image = jnp.dot(gram_sum, vector, precision=lax.Precision.HIGHEST)
        top = jnp.sqrt(jnp.sum(image * image) + 1e-06)
        vector = image / top
    return top


def chebyshev(gram_sum, damping, right_side):
    radius = top_estimate(gram_sum)
    center = damping + radius

    def operate(field):
        return jnp.dot(gram_sum, field, precision=lax.Precision.HIGHEST) + damping * field

    stride = 1.0 / center
    direction = right_side
    solution = stride * direction
    residual = right_side - stride * operate(direction)
    for sweep in range(1, ITERS):
        if sweep == 1:
            momentum = 0.5 * (radius * stride) ** 2
        else:
            momentum = (0.5 * radius * stride) ** 2
        stride = 1.0 / (center - momentum / stride)
        direction = residual + momentum * direction
        solution = solution + stride * direction
        if sweep + 1 < ITERS:
            residual = residual - stride * operate(direction)
    return solution


def self_product(rows):
    return lax.dot_general(rows, rows, (((0,), (0,)), ((), ())), preferred_element_type=jnp.float32)


def shards(activations, out_grads, proj_act, proj_out):
    examples = activations.shape[0] // SEQ
    act_low = jnp.dot(activations, proj_act, preferred_element_type=jnp.float32).astype(
        jnp.bfloat16
    )
    grad_low = jnp.dot(out_grads, proj_out, preferred_element_type=jnp.float32).astype(jnp.bfloat16)
    features = jnp.einsum(
        "etr,ets->ers",
        act_low.reshape(examples, SEQ, -1),
        grad_low.reshape(examples, SEQ, -1),
        preferred_element_type=jnp.float32,
    )
    features = features.astype(jnp.bfloat16).reshape(examples, -1)
    block_rows = core_and_chips(features, (("blk_0", "blk_1"), "blk_2"), (0, 1), 1, 0)
    width = block_rows.shape[1]
    widened = block_rows.astype(jnp.float32)
    total = one_axis_at_a_time(jnp.sum(widened * widened), GRP_BLK)
    gram_sum = self_product(lax.all_gather(block_rows, "grp", axis=0, tiled=True))
    damping = damping_rate * total / (width * lax.axis_size(BLK))
    right_side = block_rows.T.astype(jnp.float32)
    solved = chebyshev(gram_sum, damping, right_side).astype(jnp.bfloat16)
    scores = sum_at_owner(jnp.dot(block_rows, solved, preferred_element_type=jnp.float32), BLK, 0)
    return scores * float(examples * lax.axis_size("grp"))


def solution(mesh):
    split = Mesh(
        mesh.devices.reshape(mesh.shape["grp"], 4, 4, 2), ("grp", "blk_0", "blk_1", "blk_2")
    )
    placed = (P(GRP_BLK, None), P(GRP_BLK, None), P(), P())
    return jax.shard_map(
        shards, mesh=split, in_specs=placed, out_specs=P(GRP_BLK, None), check_vma=False
    )
```

profile of v0, /device:TPU:1, one launch (start us, length us, event | category | flops | bytes accessed | tf_op | source)
XLA Modules:
  0.0 180.0 jit_solution(9922667226853044475)
XLA Ops:
  6.5 4.9 %convolution_convert_fusion.2 = bf16[1024,128]{1,0:T(8,128)(2,1)S(1)} fusion(bf16[1024,3072]{1,0:T(8,128)(2,1)} %param.4, bf16[3072,128]{1,0:T(8,128)(2,1)} %param.6), kind=kOutput, calls=%fused_computation.19 | convolution fusion | flops 805437440 | bytes 7340032 | tf_op jit(solution)/shard_map/dot_general | solution.py:95
  11.8 1.8 convolution_convert_fusion.1
  14.1 1.5 reshape_reshape.6
  15.6 1.8 %copy.12 = bf16[16,32,1024]{2,0,1:T(8,128)(2,1)S(1)} copy(bf16[16,32,1024]{2,1,0:T(8,128)(2,1)} %reshape_reshape.6) | data formatting | bytes 2097152 | tf_op jit(solution)/shard_map/reshape;reshape | solution.py:18
  17.4 24.5 %all_to_all.15 = bf16[16,2,16,1024]{3,2,1,0:T(8,128)(2,1)S(1)} all-to-all(bf16[16,2,16,1024]{3,2,1,0:T(8,128)(2,1)S(1)} %bitcast.84), channel_id=1, replica_groups=mesh['grp'=4,'blk_0'=4,'blk_1'=4,'blk_2'=2] {'blk_0','blk_1'}, dimensions={0} | all-to-all | bytes 2097152 | tf_op jit(solution)/shard_map/all_to_all | solution.py:32
  42.0 6.2 %all_to_all.16 = bf16[16,2,16,1024]{3,2,0,1:T(8,128)(2,1)S(1)} all-to-all(bf16[16,2,16,1024]{3,2,0,1:T(8,128)(2,1)S(1)} %copy.13), channel_id=1, replica_groups=mesh['grp'=4,'blk_0'=4,'blk_1'=4,'blk_2'=2] {'blk_2'}, dimensions={1} | all-to-all | bytes 2097152 | tf_op jit(solution)/shard_map/all_to_all | solution.py:32
  48.2 1.0 copy-done.4
  49.2 1.1 copy.14
  50.3 2.5 %multiply_reduce_fusion = f32[]{:T(128)} fusion(bf16[16,2,16,1024]{3,2,0,1:T(8,128)(2,1)} %copy-done.4), kind=kLoop, calls=%fused_computation.13 | loop fusion | flops 1572863 | bytes 1048580 | tf_op jit(solution)/shard_map/reduce_sum | solution.py:109
  52.8 9.1 %psum.28 = f32[]{:T(128)} all-reduce(f32[]{:T(128)} %multiply_reduce_fusion), channel_id=1, replica_groups=mesh['grp'=4,'blk_0'=4,'blk_1'=4,'blk_2'=2] {'grp'}, use_global_device_ids=true, to_apply=%region_1.0 | all-reduce | flops 1 | bytes 8 | tf_op jit(solution)/shard_map/psum | solution.py:44
  61.9 8.0 %psum.29 = f32[]{:T(128)} all-reduce(f32[]{:T(128)} %psum.28), channel_id=1, replica_groups=mesh['grp'=4,'blk_0'=4,'blk_1'=4,'blk_2'=2] {'blk_0'}, use_global_device_ids=true, to_apply=%region_2.0 | all-reduce | flops 1 | bytes 8 | tf_op jit(solution)/shard_map/psum | solution.py:44
  69.8 8.0 %psum.30 = f32[]{:T(128)} all-reduce(f32[]{:T(128)} %psum.29), channel_id=1, replica_groups=mesh['grp'=4,'blk_0'=4,'blk_1'=4,'blk_2'=2] {'blk_1'}, use_global_device_ids=true, to_apply=%region_3.0 | all-reduce | flops 1 | bytes 8 | tf_op jit(solution)/shard_map/psum | solution.py:44
  77.8 7.6 %psum.31 = f32[]{:T(128)} all-reduce(f32[]{:T(128)} %psum.30), channel_id=1, replica_groups=mesh['grp'=4,'blk_0'=4,'blk_1'=4,'blk_2'=2] {'blk_2'}, use_global_device_ids=true, to_apply=%region_4.0 | all-reduce | flops 1 | bytes 8 | tf_op jit(solution)/shard_map/psum | solution.py:44
  85.4 1.3 copy.16
  87.4 8.6 %all-gather.2.cloned.1.call-done = bf16[2048,1024]{1,0:T(8,128)(2,1)} async-done(((bf16[512,1024]{1,0:T(8,128)(2,1)}), bf16[2048,1024]{1,0:T(8,128)(2,1)}) %all-gather.2.cloned.1.call-update) | async-done | bytes 4194320 | tf_op jit(solution)/shard_map/all_gather | solution.py:110
  95.9 7.8 %fusion.23 = f32[1024,1024]{1,0:T(8,128)S(1)} fusion(bf16[2048,1024]{1,0:T(8,128)(2,1)} %all-gather.2.cloned.1.call-done), kind=kOutput, calls=%fused_computation.37 | convolution fusion | flops 4294967296 | bytes 8388608 | tf_op jit(solution)/shard_map/dot_general | solution.py:90
  103.7 3.6 %fusion.20 = f32[1,1024]{1,0:T(1,128)S(1)} fusion(f32[1024,1024]{1,0:T(8,128)S(1)} %fusion.23), kind=kOutput, calls=%fused_computation.32 | convolution fusion | flops 12582912 | bytes 4198400 | tf_op jit(solution)/shard_map/dot_general | solution.py:59
  107.3 4.8 %fusion.26 = f32[1024,512]{1,0:T(8,128)} fusion(f32[1024,1024]{1,0:T(8,128)S(1)} %fusion.23, bf16[512,1024]{1,0:T(8,128)(2,1)S(1)} %bitcast.82), kind=kOutput, calls=%fused_computation.40 | convolution fusion | flops 6442450944 | bytes 7340032 | tf_op jit(solution)/shard_map/dot_general | solution.py:70
  113.4 5.8 %fusion.24 = f32[1,1024]{1,0:T(1,128)S(1)} fusion(f32[1024,1024]{1,0:T(8,128)} %copy-done.1, f32[1024,1]{0,1:T(1,128)S(1)} %bitcast.91), kind=kOutput, calls=%fused_computation.38 | convolution fusion | flops 12582912 | bytes 4202496 | tf_op jit(solution)/shard_map/dot_general | solution.py:59
  120.5 6.0 %fusion.25 = f32[1,1024]{1,0:T(1,128)S(1)} fusion(f32[1024,1024]{1,0:T(8,128)} %copy-done.1, f32[1024,1]{0,1:T(1,128)S(1)} %bitcast.92), kind=kOutput, calls=%fused_computation.39 | convolution fusion | flops 12582912 | bytes 4202496 | tf_op jit(solution)/shard_map/dot_general | solution.py:59
  128.0 9.5 %fusion.8 = f32[1024,512]{1,0:T(8,128)S(1)} fusion(f32[1024,1024]{1,0:T(8,128)} %copy-done.1, bf16[512,1024]{0,1:T(8,128)(2,1)} %copy.16, f32[1024,512]{1,0:T(8,128)} %fusion.26, f32[]{:T(128)S(6)} %mul.111, f32[]{:T(128)S(6)} %div.36, f32[]{:T(128)S(6)} %div.41), kind=kOutput, calls=%fused_computation.15 | convolution fusion | flops 6446120960 | bytes 9437196 | tf_op jit(solution)/shard_map/dot_general | solution.py:70
  137.6 9.5 %fusion.11 = bf16[1024,512,1]{1,0,2:T(8,128)(2,1)S(1)} fusion(f32[1024,1024]{1,0:T(8,128)S(1)} %copy-done.2, f32[1024,512]{1,0:T(8,128)S(1)} %fusion.8, bf16[512,1024]{0,1:T(8,128)(2,1)S(1)} %copy-done.6, f32[1024,512]{1,0:T(8,128)S(1)} %copy-done.5, f32[]{:T(128)S(6)} %integer_pow.11, f32[]{:T(128)S(6)} %div.47, f32[]{:T(128)S(6)} %integer_pow.10, ...), kind=kOutput, calls=%fused_computation.17 | convolution fusion | flops 6463422464 | bytes 10485792 | tf_op jit(solution)/shard_map/dot_general | solution.py:70
  147.1 0.7 fusion.27
  147.8 24.6 %all_to_all.17 = f32[32,16,512]{2,1,0:T(8,128)S(1)} all-to-all(f32[32,16,512]{2,1,0:T(8,128)S(1)} %fusion.27), channel_id=1, replica_groups=mesh['grp'=4,'blk_0'=4,'blk_1'=4,'blk_2'=2] {'blk_0','blk_1','blk_2'}, dimensions={0} | all-to-all | bytes 2097152 | tf_op jit(solution)/shard_map/all_to_all | solution.py:50
  (26 shorter events, 3.6 us)
Async XLA Ops:
  6.5 4.9 %copy-start = (bf16[3072,256]{1,0:T(8,128)(2,1)S(1)}, bf16[3072,256]{1,0:T(8,128)(2,1)}, u32[]{:S(2)}) copy-start(bf16[3072,256]{1,0:T(8,128)(2,1)} %param.7) | copy-start | bytes 4718596
  6.5 89.4 %all-gather.2.cloned.1.call-start = ((), (), s32[]{:S(2)}) async-start(), calls=%async_computation.3 | async-start | bytes 5242880 | tf_op jit(solution)/shard_map/all_gather | solution.py:110
  6.5 5.3 %copy-start.7 = (bf16[1024,3072]{1,0:T(8,128)(2,1)S(1)}, bf16[1024,3072]{1,0:T(8,128)(2,1)}, u32[]{:S(2)}) copy-start(bf16[1024,3072]{1,0:T(8,128)(2,1)} %param.5) | copy-start | bytes 18874372
  48.2 1.0 copy-start.4
  50.3 35.1 %copy-start.3 = (bf16[16,2,16,1024]{3,2,1,0:T(8,128)(2,1)S(1)}, bf16[16,2,16,1024]{3,2,1,0:T(8,128)(2,1)}, u32[]{:S(2)}) copy-start(bf16[16,2,16,1024]{3,2,1,0:T(8,128)(2,1)} %copy.14) | copy-start | bytes 3145732
  103.7 3.6 %copy-start.1 = (f32[1024,1024]{1,0:T(8,128)}, f32[1024,1024]{1,0:T(8,128)S(1)}, u32[]{:S(2)}) copy-start(f32[1024,1024]{1,0:T(8,128)S(1)} %fusion.23) | copy-start | bytes 12582916
  128.0 9.6 %copy-start.2 = (f32[1024,1024]{1,0:T(8,128)S(1)}, f32[1024,1024]{1,0:T(8,128)}, u32[]{:S(2)}) copy-start(f32[1024,1024]{1,0:T(8,128)} %copy-done.1) | copy-start | bytes 12582916
  128.0 9.6 %copy-start.5 = (f32[1024,512]{1,0:T(8,128)S(1)}, f32[1024,512]{1,0:T(8,128)}, u32[]{:S(2)}) copy-start(f32[1024,512]{1,0:T(8,128)} %fusion.26) | copy-start | bytes 6291460
  128.0 9.6 %copy-start.6 = (bf16[512,1024]{0,1:T(8,128)(2,1)S(1)}, bf16[512,1024]{0,1:T(8,128)(2,1)}, u32[]{:S(2)}) copy-start(bf16[512,1024]{0,1:T(8,128)(2,1)} %copy.16) | copy-start | bytes 3145732
Sparse Core Ops, SparseCore 0:
  50.4 45.4 all-gather.1
where the time goes:
time: 180 us
  blocking collectives  87.9 us (49%)
  matrix products  54.8 us (30%)
  between operations  16.4 us (9%)
  waiting for transfers between devices  8.57 us (5%)
  local copies, waits for them, and re-layouts  7.22 us (4%)
  other arithmetic  4.99 us (3%)
    psum x4, blocking collectives, one_axis_at_a_time(): array = lax.psum(array, axis)  32.6 us
    all_to_all x2, blocking collectives, moved_by_axis(): lax.all_to_all(blocks, axes[k], split_axis=k, concat_axis=k, tiled=True)  30.7 us
    all_to_all x1, blocking collectives, sum_at_owner(): blocks = lax.all_to_all(split_up(array, dim, size), axis, 0, 0, tiled=True)  24.6 us
    dot_general x3, matrix products, operate(): jnp.dot(gram_sum, field, precision=lax.Precision.HIGHEST) + damping * field  23.9 us
    dot_general x3, matrix products, top_estimate(): image = jnp.dot(gram_sum, vector, precision=lax.Precision.HIGHEST)  15.3 us
    all_gather x1, waiting for transfers between devices, shards(): lax.all_gather(block_rows, 'grp', axis=0, tiled=True)  8.55 us
    dot_general x1, matrix products, self_product(): lax.dot_general(rows, rows, (((0,), (0,)), ((), ())), preferred_element_t...  7.76 us
    dot_general x1, matrix products, shards(): jnp.dot(activations, proj_act, preferred_element_type=jnp.float32)  4.88 us
  transfers between devices with their start and end apart: 1, of which 1 were waited for; matrix products, arithmetic and copies ran while one was open for 2% of the time, Pallas kernels for 0%

commit v1 on v0

--- a/solution.py
+++ b/solution.py
@@ -107,7 +107,11 @@
     width = block_rows.shape[1]
     widened = block_rows.astype(jnp.float32)
     total = one_axis_at_a_time(jnp.sum(widened * widened), GRP_BLK)
-    gram_sum = self_product(lax.all_gather(block_rows, "grp", axis=0, tiled=True))
+    gram_sum = self_product(
+        jnp.concatenate(
+            lax.all_to_all(jnp.stack([block_rows] * lax.axis_size("grp")), "grp", 0, 0), axis=0
+        )
+    )
     damping = damping_rate * total / (width * lax.axis_size(BLK))
     right_side = block_rows.T.astype(jnp.float32)
     solved = chebyshev(gram_sum, damping, right_side).astype(jnp.bfloat16)

time: 180 us -> 200 us (1.11)
  blocking collectives: 87.9 us -> 122 us
  between operations: 16.4 us -> 3.08 us
  waiting for transfers between devices: 8.57 us -> 0.01 us
  starting transfers between devices: 0.01 us -> 4.86 us
    psum x4, blocking collectives: 32.6 us -> 71.2 us  [one_axis_at_a_time(): array = lax.psum(array, axis)]
    all_gather x1 -> x0, waiting for transfers between devices: 8.55 us -> none  [shards(): lax.all_gather(block_rows, 'grp', axis=0, tiled=True)]
    all_to_all x0 -> x1, starting transfers between devices: none -> 4.86 us  [shards(): lax.all_to_all(jnp.stack([block_rows] * lax.axis_size('grp')), 'grp', 0, 0)]
    all_to_all x1, blocking collectives: 24.6 us -> 20.5 us  [sum_at_owner(): blocks = lax.all_to_all(split_up(array, dim, size), axis, 0, 0, tiled=True)]
    another operation x1 -> x2, local copies, waits for them, and re-layouts: 1.34 us -> 3.91 us  [shards(): jnp.stack([block_rows] * lax.axis_size('grp'))]
  transfers between devices with their start and end apart: 1 -> 1, of which waited for: 1 -> 0; matrix products, arithmetic and copies ran while one was open for 2% -> 2% of each run, Pallas kernels for 0% -> 0%
where the time goes in v1:
time: 200 us; the launch traced here: 199 us
  blocking collectives  122 us (61%)
  matrix products  54.9 us (27%)
  local copies, waits for them, and re-layouts  8.83 us (4%)
  other arithmetic  4.9 us (2%)
  starting transfers between devices  4.86 us (2%)
  between operations  3.08 us (2%)
    psum x4, blocking collectives, one_axis_at_a_time(): array = lax.psum(array, axis)  71.2 us
    all_to_all x2, blocking collectives, moved_by_axis(): lax.all_to_all(blocks, axes[k], split_axis=k, concat_axis=k, tiled=True)  30.7 us
    dot_general x3, matrix products, operate(): jnp.dot(gram_sum, field, precision=lax.Precision.HIGHEST) + damping * field  23.9 us
    all_to_all x1, blocking collectives, sum_at_owner(): blocks = lax.all_to_all(split_up(array, dim, size), axis, 0, 0, tiled=True)  20.5 us
    dot_general x3, matrix products, top_estimate(): image = jnp.dot(gram_sum, vector, precision=lax.Precision.HIGHEST)  15.3 us
    dot_general x1, matrix products, self_product(): lax.dot_general(rows, rows, (((0,), (0,)), ((), ())), preferred_element_t...  7.77 us
    dot_general x1, matrix products, shards(): jnp.dot(activations, proj_act, preferred_element_type=jnp.float32)  4.87 us
    all_to_all x1, starting transfers between devices, shards(): lax.all_to_all(jnp.stack([block_rows] * lax.axis_size('grp')), 'grp', 0, 0)  4.86 us
  transfers between devices with their start and end apart: 1, of which 0 were waited for; matrix products, arithmetic and copies ran while one was open for 2% of the time, Pallas kernels for 0%

profile of v1, /device:TPU:1, one launch (start us, length us, event | category | flops | bytes accessed | tf_op | source)
XLA Modules:
  0.0 199.0 jit_solution(7071030417908760595)
XLA Ops:
  0.0 4.9 %convolution_convert_fusion.2 = bf16[1024,128]{1,0:T(8,128)(2,1)S(1)} fusion(bf16[1024,3072]{1,0:T(8,128)(2,1)} %param.4, bf16[3072,128]{1,0:T(8,128)(2,1)} %param.6), kind=kOutput, calls=%fused_computation.29 | convolution fusion | flops 805437440 | bytes 7340032 | tf_op jit(solution)/shard_map/dot_general | solution.py:95
  5.3 1.8 convolution_convert_fusion.1
  7.6 1.5 reshape_reshape.4
  9.1 1.8 copy.16
  10.9 24.5 %all_to_all.20 = bf16[16,2,16,1024]{3,2,1,0:T(8,128)(2,1)S(1)} all-to-all(bf16[16,2,16,1024]{3,2,1,0:T(8,128)(2,1)S(1)} %bitcast.95), channel_id=1, replica_groups=mesh['grp'=4,'blk_0'=4,'blk_1'=4,'blk_2'=2] {'blk_0','blk_1'}, dimensions={0} | all-to-all | bytes 2097152 | tf_op jit(solution)/shard_map/all_to_all | solution.py:32
  35.5 6.2 %all_to_all.21 = bf16[16,2,16,1024]{3,2,0,1:T(8,128)(2,1)S(1)} all-to-all(bf16[16,2,16,1024]{3,2,0,1:T(8,128)(2,1)S(1)} %copy.17), channel_id=1, replica_groups=mesh['grp'=4,'blk_0'=4,'blk_1'=4,'blk_2'=2] {'blk_2'}, dimensions={1} | all-to-all | bytes 2097152 | tf_op jit(solution)/shard_map/all_to_all | solution.py:32
  41.7 1.1 copy-done.3
  42.8 2.5 %stack.3 = bf16[4,512,1024]{2,1,0:T(8,128)(2,1)} broadcast(bf16[512,1024]{1,0:T(8,128)(2,1)S(1)} %bitcast.91), dimensions={1,2} | broadcast | bytes 5242880 | tf_op jit(solution)/shard_map/stack | solution.py:112
  45.3 4.9 %all-to-all-start.2 = ((bf16[4,512,1024]{2,1,0:T(8,128)(2,1)}), bf16[4,512,1024]{2,1,0:T(8,128)(2,1)}, u32[]{:S(2)}, u32[]{:S(2)}) async-start(bf16[4,512,1024]{2,1,0:T(8,128)(2,1)} %stack.3), calls=%async_computation.2 | async-start | bytes 8388608 | tf_op jit(solution)/shard_map/all_to_all | solution.py:112
  50.2 2.4 %multiply_reduce_fusion = f32[]{:T(128)} fusion(bf16[16,2,16,1024]{3,2,0,1:T(8,128)(2,1)} %copy-done.3), kind=kLoop, calls=%fused_computation.25 | loop fusion | flops 1572863 | bytes 1048580 | tf_op jit(solution)/shard_map/reduce_sum | solution.py:109
  52.6 48.1 %psum.28 = f32[]{:T(128)} all-reduce(f32[]{:T(128)} %multiply_reduce_fusion), channel_id=1, replica_groups=mesh['grp'=4,'blk_0'=4,'blk_1'=4,'blk_2'=2] {'grp'}, use_global_device_ids=true, to_apply=%region_1.0 | all-reduce | flops 1 | bytes 8 | tf_op jit(solution)/shard_map/psum | solution.py:44
  100.7 7.2 %psum.29 = f32[]{:T(128)} all-reduce(f32[]{:T(128)} %psum.28), channel_id=1, replica_groups=mesh['grp'=4,'blk_0'=4,'blk_1'=4,'blk_2'=2] {'blk_0'}, use_global_device_ids=true, to_apply=%region_2.0 | all-reduce | flops 1 | bytes 8 | tf_op jit(solution)/shard_map/psum | solution.py:44
  107.9 7.2 %psum.30 = f32[]{:T(128)} all-reduce(f32[]{:T(128)} %psum.29), channel_id=1, replica_groups=mesh['grp'=4,'blk_0'=4,'blk_1'=4,'blk_2'=2] {'blk_1'}, use_global_device_ids=true, to_apply=%region_3.0 | all-reduce | flops 1 | bytes 8 | tf_op jit(solution)/shard_map/psum | solution.py:44
  115.1 8.7 %psum.31 = f32[]{:T(128)} all-reduce(f32[]{:T(128)} %psum.30), channel_id=1, replica_groups=mesh['grp'=4,'blk_0'=4,'blk_1'=4,'blk_2'=2] {'blk_2'}, use_global_device_ids=true, to_apply=%region_4.0 | all-reduce | flops 1 | bytes 8 | tf_op jit(solution)/shard_map/psum | solution.py:44
  123.8 1.4 copy.21
  125.9 7.8 %fusion.36 = f32[1024,1024,1]{1,0,2:T(8,128)S(1)} fusion(bf16[4,512,1024]{2,1,0:T(8,128)(2,1)} %all-to-all-done.2), kind=kOutput, calls=%fused_computation.46 | convolution fusion | flops 4294967296 | bytes 8388608 | tf_op jit(solution)/shard_map/dot_general | solution.py:90
  133.7 3.6 %fusion.10 = f32[1,1024]{1,0:T(1,128)S(1)} fusion(f32[1024,1024,1]{1,0,2:T(8,128)S(1)} %fusion.36), kind=kOutput, calls=%fused_computation.10 | convolution fusion | flops 12582912 | bytes 4198400 | tf_op jit(solution)/shard_map/dot_general | solution.py:59
  137.3 4.8 %fusion.4 = f32[1024,512]{1,0:T(8,128)} fusion(bf16[512,1024]{1,0:T(8,128)(2,1)S(1)} %bitcast.93, f32[1024,1024,1]{1,0,2:T(8,128)S(1)} %fusion.36), kind=kOutput, calls=%fused_computation.4 | convolution fusion | flops 6442450944 | bytes 7340032 | tf_op jit(solution)/shard_map/dot_general | solution.py:70
  143.4 5.8 %fusion.8 = f32[1,1024]{1,0:T(1,128)S(1)} fusion(f32[1024,1]{0,1:T(1,128)S(1)} %bitcast.102, f32[1024,1024,1]{1,0,2:T(8,128)} %copy-done.1), kind=kOutput, calls=%fused_computation.8 | convolution fusion | flops 12582912 | bytes 4202496 | tf_op jit(solution)/shard_map/dot_general | solution.py:59
  150.4 6.0 %fusion.6 = f32[1,1024]{1,0:T(1,128)S(1)} fusion(f32[1024,1]{0,1:T(1,128)S(1)} %bitcast.103, f32[1024,1024,1]{1,0,2:T(8,128)} %copy-done.1), kind=kOutput, calls=%fused_computation.6 | convolution fusion | flops 12582912 | bytes 4202496 | tf_op jit(solution)/shard_map/dot_general | solution.py:59
  157.9 9.5 %fusion.2 = f32[1024,512]{1,0:T(8,128)S(1)} fusion(f32[1024,1024,1]{1,0,2:T(8,128)} %copy-done.1, bf16[512,1024]{0,1:T(8,128)(2,1)} %copy.21, f32[1024,512]{1,0:T(8,128)} %fusion.4, f32[]{:T(128)S(6)} %mul.111, f32[]{:T(128)S(6)} %div.36, f32[]{:T(128)S(6)} %div.41), kind=kOutput, calls=%fused_computation.2 | convolution fusion | flops 6446120960 | bytes 9437196 | tf_op jit(solution)/shard_map/dot_general | solution.py:70
  167.5 9.6 %fusion.23 = bf16[1024,512,1]{1,0,2:T(8,128)(2,1)S(1)} fusion(f32[1024,512]{1,0:T(8,128)S(1)} %fusion.2, bf16[512,1024]{0,1:T(8,128)(2,1)S(1)} %copy-done.5, f32[1024,512]{1,0:T(8,128)S(1)} %copy-done.4, f32[1024,1024,1]{1,0,2:T(8,128)S(1)} %copy-done.2, f32[]{:T(128)S(6)} %integer_pow.11, f32[]{:T(128)S(6)} %div.47, f32[]{:T(128)S(6)} %integer_pow.10, ...), kind=kOutput, calls=%fused_computation.27 | convolution fusion | flops 6463422464 | bytes 10485792 | tf_op jit(solution)/shard_map/dot_general | solution.py:70
  177.1 0.7 fusion.37
  177.8 20.5 %all_to_all.22 = f32[32,16,512]{2,1,0:T(8,128)S(1)} all-to-all(f32[32,16,512]{2,1,0:T(8,128)S(1)} %fusion.37), channel_id=1, replica_groups=mesh['grp'=4,'blk_0'=4,'blk_1'=4,'blk_2'=2] {'blk_0','blk_1','blk_2'}, dimensions={0} | all-to-all | bytes 2097152 | tf_op jit(solution)/shard_map/all_to_all | solution.py:50
  (24 shorter events, 3.6 us)
Async XLA Ops:
  0.0 4.9 %copy-start = (bf16[3072,256]{1,0:T(8,128)(2,1)S(1)}, bf16[3072,256]{1,0:T(8,128)(2,1)}, u32[]{:S(2)}) copy-start(bf16[3072,256]{1,0:T(8,128)(2,1)} %param.7) | copy-start | bytes 4718596
  0.0 5.3 %copy-start.6 = (bf16[1024,3072]{1,0:T(8,128)(2,1)S(1)}, bf16[1024,3072]{1,0:T(8,128)(2,1)}, u32[]{:S(2)}) copy-start(bf16[1024,3072]{1,0:T(8,128)(2,1)} %param.5) | copy-start | bytes 18874372
  41.7 1.1 copy-start.3
  45.3 80.5 %all-to-all-start.2 = ((bf16[4,512,1024]{2,1,0:T(8,128)(2,1)}), bf16[4,512,1024]{2,1,0:T(8,128)(2,1)}, u32[]{:S(2)}, u32[]{:S(2)}) async-start(bf16[4,512,1024]{2,1,0:T(8,128)(2,1)} %stack.3), calls=%async_computation.2 | async-start | bytes 8388608 | tf_op jit(solution)/shard_map/all_to_all | solution.py:112
  133.6 3.6 %copy-start.1 = (f32[1024,1024,1]{1,0,2:T(8,128)}, f32[1024,1024,1]{1,0,2:T(8,128)S(1)}, u32[]{:S(2)}) copy-start(f32[1024,1024,1]{1,0,2:T(8,128)S(1)} %fusion.36) | copy-start | bytes 12582916
  157.9 9.6 %copy-start.2 = (f32[1024,1024,1]{1,0,2:T(8,128)S(1)}, f32[1024,1024,1]{1,0,2:T(8,128)}, u32[]{:S(2)}) copy-start(f32[1024,1024,1]{1,0,2:T(8,128)} %copy-done.1) | copy-start | bytes 12582916
  157.9 9.6 %copy-start.4 = (f32[1024,512]{1,0:T(8,128)S(1)}, f32[1024,512]{1,0:T(8,128)}, u32[]{:S(2)}) copy-start(f32[1024,512]{1,0:T(8,128)} %fusion.4) | copy-start | bytes 6291460
  157.9 9.6 %copy-start.5 = (bf16[512,1024]{0,1:T(8,128)(2,1)S(1)}, bf16[512,1024]{0,1:T(8,128)(2,1)}, u32[]{:S(2)}) copy-start(bf16[512,1024]{0,1:T(8,128)(2,1)} %copy.21) | copy-start | bytes 3145732
